TPU v7x, 128 devices: a whole 4x4x4 slice. The times are simulated.
128 devices in a mesh: grp: 8 (over x, core), inner: 16 (over z, y).
Axes of the slice: x: 4, y: 4, z: 4, core: 2. Of those that a mesh axis runs over, the one named last changes fastest.
Arguments:
- moe_input: bfloat16 [16384, 2048], P(('grp', 'inner')), may hold values from -6 to 6
- out_grad: bfloat16 [16384, 2048], P(('grp', 'inner')), may hold values from -1.5 to 1.5
- context: bfloat16 [16384, 4096], P('grp', 'inner'), may hold values from -0.119628906 to 0.119628906
- gate_scale: float32 [128, 256], P(('grp', 'inner')), may hold values from 0.2 to 1
- selected: int32 [128, 256], replicated, may hold values from 0 to 16383, as said below
- w_gate: bfloat16 [128, 2048, 768], P(('grp', 'inner')), may hold values from -0.125 to 0.125
- w_up: bfloat16 [128, 2048, 768], P(('grp', 'inner')), may hold values from -0.125 to 0.125
- w_down: bfloat16 [128, 768, 2048], P(('grp', 'inner')), may hold values from -0.21875 to 0.21875
- w_out: bfloat16 [4096, 2048], P('inner'), may hold values from -0.09375 to 0.09375
Outputs:
- grad_gate: bfloat16 [128, 2048, 768], P(('grp', 'inner'))
- grad_up: bfloat16 [128, 2048, 768], P(('grp', 'inner'))
- grad_down: bfloat16 [128, 768, 2048], P(('grp', 'inner'))
- grad_context: bfloat16 [16384, 4096], P('grp', 'inner')
- grad_out: bfloat16 [4096, 2048], P('inner', 'grp')
Inputs may be any that keep to these rules, and one draw needn't show every extreme that they name: `selected`: each expert's 256 token indices are distinct; at most 4 of them lie among the 128 tokens of one device (tokens d * 128 to (d + 1) * 128 - 1), and every expert takes exactly 4 from some device.
All inputs are finite; a program needn't handle non-finite values.
Results may differ from a plain program's by a relative error of at most 0.014.
Values may be sent and summed in bfloat16 or wider, within the bound.
No kernel may reach another device: no remote copies, remote signals or barrier semaphores. Data moves between devices by JAX's collectives and lax.ppermute only.
A program may use at most 128 MiB of HBM per device.

v0:
```python
import jax
import jax.numpy as jnp
from jax import lax
from jax.experimental import pallas as pl
from jax.experimental.pallas import tpu as pltpu
from jax.sharding import PartitionSpec as P


F32 = jnp.float32
BF16 = jnp.bfloat16
ROWS = (((0,), (0,)), ((), ()))
LAST = (((1,), (1,)), ((), ()))
SIDE = 4


def dot(left, right, dims=(((1,), (0,)), ((), ()))):
    return lax.dot_general(left, right, dims, preferred_element_type=F32)


def ring_pairs(step, along_z):
    pairs = []
    for z in range(SIDE):
        for y in range(SIDE):
            to = ((z + step) % SIDE) * SIDE + y if along_z else z * SIDE + (y + step) % SIDE
            pairs.append((z * SIDE + y, to))
    return pairs


def core_pairs():
    return [(2 * x + core, 2 * x + 1 - core) for x in range(SIDE) for core in range(2)]


def x_pairs(step):
    return [(2 * x + core, 2 * ((x + step) % SIDE) + core) for x in range(SIDE) for core in range(2)]


def ahead(block, step, along_z):
    return lax.ppermute(block, "inner", ring_pairs(-step, along_z))


def cost(flops, moved):
    return pl.CostEstimate(flops=flops, bytes_accessed=moved, transcendentals=0)


def small(limit):
    return pltpu.CompilerParams(vmem_limit_bytes=limit * 1024 * 1024)


def pick_kernel(device, selected, moe_input, out_grad, out, table_out, picker, rows):
    step = pl.program_id(0)
    experts, slots = selected.shape
    tokens, lanes = moe_input.shape[0], table_out.shape[1]

    @pl.when(step == 0)
    def _():
        rel = selected[...] - device[0] * tokens
        mine = (rel >= 0) & (rel < tokens)
        first = lax.broadcasted_iota(jnp.int32, (slots, slots), 0)
        second = lax.broadcasted_iota(jnp.int32, (slots, slots), 1)
        order = dot(
            jnp.where(mine, 1.0, 0.0).astype(BF16),
            jnp.where(first <= second, 1.0, 0.0).astype(BF16),
        )
        lane = lax.broadcasted_iota(jnp.int32, (experts, lanes), 1)
        number = (rel + 1).astype(F32)
        table = jnp.zeros((experts, lanes), F32)
        for k in range(4):
            hit = mine & (order == k + 1.0)
            value = jnp.sum(jnp.where(hit, number, 0.0), axis=1, keepdims=True)
            table = jnp.where(lane == k, value, table)
            table = jnp.where((lane == k + 4) & (value > 0.0), value + tokens, table)
        table_out[...] = table
        row = lax.broadcasted_iota(jnp.int32, (8 * experts, lanes), 0)
        lane = lax.broadcasted_iota(jnp.int32, (8 * experts, lanes), 1)
        spread = dot(jnp.where(row // 8 == lane, 1.0, 0.0).astype(BF16), table.astype(BF16))
        pick = jnp.sum(jnp.where(lane == row % 8, spread, 0.0), axis=1, keepdims=True)
        token = lax.broadcasted_iota(jnp.int32, picker.shape, 1) + 1
        picker[...] = jnp.where(token.astype(F32) == pick, 1.0, 0.0).astype(BF16)
        rows[:tokens, :] = moe_input[...]
        rows[tokens:, :] = out_grad[...]

    size = out.shape[0]
    part = picker[pl.ds(pl.multiple_of(step * size, size), size), :]
    out[...] = dot(part, rows[...]).astype(BF16)


def picked(device, selected, moe_input, out_grad):
    experts, slots = selected.shape
    tokens, width = moe_input.shape
    size = 256
    whole = pl.BlockSpec((tokens, width), lambda c: (0, 0))
    return pl.pallas_call(
        pick_kernel,
        out_shape=(
            jax.ShapeDtypeStruct((8 * experts, width), BF16),
            jax.ShapeDtypeStruct((experts, 128), F32),
        ),
        grid=(8 * experts // size,),
        in_specs=[
            pl.BlockSpec(memory_space=pltpu.SMEM),
            pl.BlockSpec((experts, slots), lambda c: (0, 0)),
            whole,
            whole,
        ],
        out_specs=(
            pl.BlockSpec((size, width), lambda c: (c, 0)),
            pl.BlockSpec((experts, 128), lambda c: (0, 0)),
        ),
        scratch_shapes=[
            pltpu.VMEM((8 * experts, 2 * tokens), BF16),
            pltpu.VMEM((2 * tokens, width), BF16),
        ],
        compiler_params=small(60),
        cost_estimate=cost(32 * experts * tokens * width, 20 * experts * width),
    )(device.reshape(1), selected, moe_input, out_grad)


def expert_kernel(position, scale, spots, gate_hbm, up_hbm, down_hbm, arrived, *refs):
    results, refs = refs[:6], refs[6:]
    chunks, gate_w, up_w, down_w, gate_sum, up_sum, back_sum, stacked = refs[:8]
    rows_in, scaled_in, hidden, back_gate, back_up, out, in_sem, out_sem = refs[8:]
    count, depth, wide = chunks.shape
    slots = position.shape[0]

    def fetches(k):
        cols = slice(k * wide, (k + 1) * wide)
        pairs = (
            (arrived.at[:, cols], chunks.at[k]),
            (gate_hbm.at[cols, :], gate_w.at[cols, :]),
            (up_hbm.at[cols, :], up_w.at[cols, :]),
            (down_hbm.at[:, cols], down_w.at[:, cols]),
        )
        return [pltpu.make_async_copy(a, b, in_sem.at[k, n]) for n, (a, b) in enumerate(pairs)]

    def store(n, source):
        return pltpu.make_async_copy(source, results[n], out_sem.at[n])

    ahead_by = 2
    for k in range(ahead_by):
        for copy in fetches(k):
            copy.start()
    spot = lax.broadcasted_iota(jnp.int32, (slots, depth), 1)
    place_in = jnp.where(spot == position[...], 1.0, 0.0).astype(BF16)
    place_grad = jnp.where(spot == position[...] + 4, 1.0, 0.0).astype(BF16)
    for k in range(count):
        cols = slice(k * wide, (k + 1) * wide)
        waits = fetches(k)
        waits[0].wait()
        chunk = chunks[k]
        rows = dot(place_in, chunk).astype(BF16)
        scaled = (dot(place_grad, chunk) * scale[...]).astype(BF16)
        rows_in[:, cols] = rows
        scaled_in[:, cols] = scaled
        for copy in waits[1:]:
            copy.wait()
        if k + ahead_by < count:
            for copy in fetches(k + ahead_by):
                copy.start()
        terms = (
            (gate_sum, dot(rows, gate_w[cols, :])),
            (up_sum, dot(rows, up_w[cols, :])),
            (back_sum, dot(scaled, down_w[:, cols], LAST)),
        )
        for total, term in terms:
            total[...] = term if k == 0 else total[...] + term
    store(0, rows_in).start()
    store(1, scaled_in).start()
    gate_pre, up_pre, back = gate_sum[...], up_sum[...], back_sum[...]
    sig = jax.nn.sigmoid(gate_pre)
    silu = gate_pre * sig
    back_gate[...] = (back * up_pre * sig * (1.0 + gate_pre * (1.0 - sig))).astype(BF16)
    back_up[...] = (back * silu).astype(BF16)
    hidden[...] = (silu * up_pre).astype(BF16)
    for n, source in ((2, hidden), (3, back_gate), (4, back_up)):
        store(n, source).start()
    half = stacked.shape[1]
    for h in range(2):
        cols = slice(h * half, (h + 1) * half)
        part = dot(back_gate[...], gate_w[cols, :], LAST) + dot(back_up[...], up_w[cols, :], LAST)
        stacked[h * slots : (h + 1) * slots, :] = part.astype(BF16)
    size = out.shape[1]

    def send(k):
        return pltpu.make_async_copy(
            out.at[k], results[5].at[k * size : (k + 1) * size, :], out_sem.at[5 + k]
        )

    for k in range(out.shape[0]):
        row = lax.broadcasted_iota(jnp.int32, (size, spots.shape[1]), 0) + k * size
        unplace = jnp.where(row == spots[...], 1.0, 0.0).astype(BF16)
        out[k] = dot(unplace, stacked[...]).astype(BF16)
        send(k).start()
    for n, source in enumerate((rows_in, scaled_in, hidden, back_gate, back_up)):
        store(n, source).wait()
    for k in range(out.shape[0]):
        send(k).wait()


def expert(position, scale, spots, gate_w, up_w, down_w, arrived):
    slots = position.shape[0]
    depth, width = arrived.shape
    hid = gate_w.shape[1]
    chunks, half = 4, width // 2
    rows, units = (slots, width), (slots, hid)
    shapes = (rows, rows, units, units, units, (depth, half))
    flops = 4 * slots * depth * width + 10 * slots * width * hid + 4 * slots * depth * half
    hbm = pl.BlockSpec(memory_space=pl.ANY)
    return pl.pallas_call(
        expert_kernel,
        out_shape=[jax.ShapeDtypeStruct(shape, BF16) for shape in shapes],
        in_specs=[pl.BlockSpec(a.shape, lambda: (0, 0)) for a in (position, scale, spots)]
        + [hbm] * 4,
        out_specs=[hbm] * 6,
        scratch_shapes=[
            pltpu.VMEM((chunks, depth, width // chunks), BF16),
            pltpu.VMEM((width, hid), BF16),
            pltpu.VMEM((width, hid), BF16),
            pltpu.VMEM((hid, width), BF16),
            pltpu.VMEM(units, F32),
            pltpu.VMEM(units, F32),
            pltpu.VMEM(units, F32),
            pltpu.VMEM((2 * slots, half), BF16),
            pltpu.VMEM(rows, BF16),
            pltpu.VMEM(rows, BF16),
            pltpu.VMEM(units, BF16),
            pltpu.VMEM(units, BF16),
            pltpu.VMEM(units, BF16),
            pltpu.VMEM((4, depth // 4, half), BF16),
            pltpu.SemaphoreType.DMA((chunks, 4)),
            pltpu.SemaphoreType.DMA((9,)),
        ],
        compiler_params=small(60),
        cost_estimate=cost(flops, 2 * depth * width + 6 * width * hid),
    )(position, scale, spots, gate_w, up_w, down_w, arrived)


def sum_kernel(table, back, own, out_a, out_b, chunks, mine, sems):
    count, rows, wide = chunks.shape
    tokens = mine.shape[0]

    def fetch(k):
        return pltpu.make_async_copy(
            back.at[:, k * wide : (k + 1) * wide], chunks.at[k], sems.at[k]
        )

    for k in range(count):
        fetch(k).start()
    first = pltpu.make_async_copy(own, mine, sems.at[count])
    first.start()
    token = lax.broadcasted_iota(jnp.int32, (tokens, rows), 0)
    row = lax.broadcasted_iota(jnp.int32, (tokens, rows), 1)
    hit = token == table[...]
    low = (row // 4) % 2 == 0
    add_a = jnp.where(hit & low, 1.0, 0.0).astype(BF16)
    add_b = jnp.where(hit & ~low, 1.0, 0.0).astype(BF16)
    first.wait()
    for k in range(count):
        fetch(k).wait()
        cols = slice(k * wide, (k + 1) * wide)
        after = slice((count + k) * wide, (count + k + 1) * wide)
        chunk = chunks[k]
        out_a[:, cols] = (mine[:, cols].astype(F32) + dot(add_a, chunk)).astype(BF16)
        out_b[:, cols] = (mine[:, after].astype(F32) + dot(add_b, chunk)).astype(BF16)


def sum_back(table, back, own):
    rows, cols = back.shape
    tokens = own.shape[0]
    count = 4
    out = jax.ShapeDtypeStruct((tokens, cols), BF16)
    hbm = pl.BlockSpec(memory_space=pltpu.HBM)
    return pl.pallas_call(
        sum_kernel,
        out_shape=(out, out),
        in_specs=[pl.BlockSpec((1, rows), lambda: (0, 0)), hbm, hbm],
        scratch_shapes=[
            pltpu.VMEM((count, rows, cols // count), BF16),
            pltpu.VMEM(own.shape, BF16),
            pltpu.SemaphoreType.DMA((count + 1,)),
        ],
        compiler_params=small(16),
        cost_estimate=cost(4 * tokens * rows * cols, 2 * rows * cols),
    )(table, back, own)


def join_kernel(a0, a1, b0, b1, a, b):
    rows = a0.shape[0]
    a[:rows, :] = a0[...]
    a[rows:, :] = a1[...]
    b[:rows, :] = b0[...]
    b[rows:, :] = b1[...]


def join(a0, a1, b0, b1):
    rows, cols = a0.shape
    out = jax.ShapeDtypeStruct((2 * rows, cols), BF16)
    return pl.pallas_call(
        join_kernel,
        out_shape=(out, out),
        compiler_params=small(16),
        cost_estimate=cost(0, 16 * rows * cols),
    )(a0, a1, b0, b1)


def turn_kernel(table, block, out_a, out_b):
    turned = block[...].T
    out_a[...] = turned
    out_b[...] = turned


def turned_context(table, context):
    tokens, heads = context.shape
    rows = tokens // 16
    out = jax.ShapeDtypeStruct((heads, tokens), BF16)
    return pl.pallas_call(
        turn_kernel,
        out_shape=(out, out),
        grid_spec=pltpu.PrefetchScalarGridSpec(
            num_scalar_prefetch=1,
            grid=(16,),
            in_specs=[pl.BlockSpec((rows, heads), lambda j, t: (t[j], 0))],
            out_specs=(
                pl.BlockSpec((heads, rows), lambda j, t: (0, j)),
                pl.BlockSpec((heads, rows), lambda j, t: (0, (j % SIDE) * SIDE + j // SIDE)),
            ),
        ),
        compiler_params=small(16),
        cost_estimate=cost(0, 6 * tokens * heads),
    )(table, context)


def ctx_rows(path, spot, rows):
    off, top = spot // 2, 2 * (spot % 2)
    if path == 0:
        return [slice((off * SIDE + top) * rows, (off * SIDE + top + 2) * rows)]
    return [slice(((top + k) * SIDE + off) * rows, ((top + k) * SIDE + off + 1) * rows) for k in range(2)]


EARLY = (0, 1, 2, 6)
MID = (3, 7)
LATE = (4, 5)


def proj_kernel(spots, with_ctx, has_before, twin, *refs):
    count = len(spots)
    refs = list(refs)
    turned = [[refs.pop(0) for _ in range(count)] for _ in range(2)]
    arrays = [[refs.pop(0) for _ in range(count)] for _ in range(2)]
    before = refs.pop(0) if has_before else None
    weights = [refs.pop(0), refs.pop(0)] if with_ctx else None
    proj = refs.pop(0)
    ctx = refs.pop(0) if with_ctx else None
    narrow = refs.pop(0) if twin else None
    rows = arrays[0][0].shape[0] // 2

    if with_ctx:

        @pl.when(pl.program_id(0) == 0)
        def _():
            ctx[...] = jnp.zeros_like(ctx)

    for path in range(2):
        total = before[path, 0] if has_before else None
        for k, spot in enumerate(spots):
            piece = arrays[path][k][...]
            term = dot(turned[path][k][...], piece)
            total = term if total is None else total + term
            if with_ctx:
                part = dot(piece, weights[path][...])
                at = 0
                for span in ctx_rows(path, spot, rows):
                    size = span.stop - span.start
                    ctx[span, :] += part[at : at + size]
                    at += size
        proj[path, 0] = total
        if twin:
            narrow[path, 0] = total.astype(BF16)


def projected(spots, turned, arrays, before=None, w_t=None, twin=False):
    heads, tokens = turned[0].shape
    depth, cols = arrays[0][0].shape
    count = len(spots)
    wide = 256
    steps = cols // wide
    slab = pl.BlockSpec((2, 1, heads, wide), lambda c: (0, c, 0, 0))
    in_specs = [pl.BlockSpec((heads, depth), lambda c, s=spot: (0, s)) for spot in spots] * 2
    in_specs += [pl.BlockSpec((depth, wide), lambda c: (0, c))] * (2 * count)
    operands = [turned[0]] * count + [turned[1]] * count + arrays[0] + arrays[1]
    out_shape = [jax.ShapeDtypeStruct((2, steps, heads, wide), F32)]
    out_specs = [slab]
    if before is not None:
        in_specs.append(slab)
        operands.append(before)
    if w_t is not None:
        in_specs.append(pl.BlockSpec((wide, heads), lambda c: (c, 0)))
        in_specs.append(pl.BlockSpec((wide, heads), lambda c: (c + steps, 0)))
        operands += [w_t, w_t]
        out_shape.append(jax.ShapeDtypeStruct((tokens, heads), F32))
        out_specs.append(pl.BlockSpec((tokens, heads), lambda c: (0, 0)))
    if twin:
        out_shape.append(jax.ShapeDtypeStruct((2, steps, heads, wide), BF16))
        out_specs.append(slab)
    flops = 4 * count * depth * heads * cols * (1 if w_t is None else 2)
    return pl.pallas_call(
        lambda *refs: proj_kernel(spots, w_t is not None, before is not None, twin, *refs),
        out_shape=out_shape,
        grid=(steps,),
        in_specs=in_specs,
        out_specs=out_specs,
        compiler_params=small(20),
        cost_estimate=cost(flops, 4 * count * depth * cols + 8 * heads * cols),
    )(*operands)


def pair_kernel(place, keep, got, own, *sent):
    x, core = place[0], place[1]
    for step in range(SIDE):
        at = (x + step) % SIDE
        path, column = at // 2, 2 * (at % 2) + core
        total = keep[path, column] + got[path, column].astype(F32)
        if step == 0:
            own[...] = total
        else:
            sent[step - 1][...] = total.astype(BF16)


def pair_sum(place, keep, got):
    heads, wide = keep.shape[2:]
    sent = jax.ShapeDtypeStruct((heads, wide), BF16)
    whole = pl.BlockSpec(keep.shape, lambda: (0, 0, 0, 0))
    return pl.pallas_call(
        pair_kernel,
        out_shape=(jax.ShapeDtypeStruct((heads, wide), F32), sent, sent, sent),
        in_specs=[pl.BlockSpec(memory_space=pltpu.SMEM), whole, whole],
        compiler_params=small(16),
        cost_estimate=cost(0, 10 * SIDE * heads * wide),
    )(place, keep, got)


def ctx_kernel(spots, table, before, w_t, *refs):
    count = len(spots)
    arrays, out = refs[: 2 * count], refs[2 * count]
    depth, cols = arrays[0].shape
    rows = depth // 2
    parts = {}
    for path in range(2):
        weights = w_t[path * cols : (path + 1) * cols, :]
        for k, spot in enumerate(spots):
            part = dot(arrays[path * count + k][...], weights)
            at = 0
            for span in ctx_rows(path, spot, rows):
                for start in range(span.start, span.stop, rows):
                    parts.setdefault(start // rows, []).append(part[at : at + rows])
                    at += rows
    for block in range(SIDE * SIDE):
        total = before[block * rows : (block + 1) * rows, :]
        for part in parts.get(block, []):
            total = total + part
        at = pl.multiple_of(table[block] * rows, rows)
        out[pl.ds(at, rows), :] = total.astype(BF16)


def ctx_rest(spots, table, before, w_t, arrays):
    tokens, heads = before.shape
    depth, cols = arrays[0][0].shape
    count = len(spots)
    operands = [before, w_t, *arrays[0], *arrays[1]]
    return pl.pallas_call(
        lambda *refs: ctx_kernel(spots, *refs),
        out_shape=jax.ShapeDtypeStruct((tokens, heads), BF16),
        in_specs=[pl.BlockSpec(memory_space=pltpu.SMEM)]
        + [pl.BlockSpec(a.shape, lambda: (0, 0)) for a in operands],
        compiler_params=small(20),
        cost_estimate=cost(4 * count * depth * heads * cols, 8 * tokens * heads),
    )(table, *operands)


def body(moe_input, out_grad, context, gate_scale, selected, w_gate, w_up, w_down, w_out):
    groups = lax.axis_size("grp")
    inner_count = lax.axis_size("inner")
    devices = groups * inner_count
    tok_rows, width = moe_input.shape
    capacity = selected.shape[1]
    most = 4
    half = width // 2
    inner = lax.axis_index("inner")
    grp = lax.axis_index("grp")
    x, core = grp // 2, grp % 2
    device = grp * inner_count + inner
    both = ("grp", "inner")

    sent, numbers = picked(device, selected, moe_input, out_grad)
    arrived = lax.all_to_all(
        sent.reshape(devices, 2 * most, width), both, split_axis=0, concat_axis=0, tiled=True
    )
    token_table = numbers[:, :most].astype(jnp.int32) - 1

    owner = selected // tok_rows
    my_owner = lax.dynamic_index_in_dim(owner, device, 0, keepdims=False)
    slot_range = jnp.arange(capacity, dtype=jnp.int32)
    same_owner = (my_owner[:, None] == my_owner[None, :]) & (
        slot_range[:, None] > slot_range[None, :]
    )
    ranking = jnp.sum(same_owner.astype(jnp.int32), axis=1)
    position = my_owner * (2 * most) + ranking
    half_of = jnp.arange(2 * capacity, dtype=jnp.int32) // capacity
    spot_of = jnp.tile(position, 2) + half_of * most
    rows_in, scaled, hidden, back_gate, back_up, placed = expert(
        position.reshape(-1, 1),
        gate_scale.reshape(-1, 1),
        spot_of.reshape(1, -1),
        w_gate[0],
        w_up[0],
        w_down[0],
        arrived.reshape(devices * 2 * most, width),
    )
    placed = placed.reshape(devices, 2 * most, half)
    returned = lax.all_to_all(placed, both, split_axis=0, concat_axis=0, tiled=True)

    grad_down = dot(hidden, scaled, ROWS).astype(BF16)
    grad_gate = dot(rows_in, back_gate, ROWS).astype(BF16)
    grad_up = dot(rows_in, back_up, ROWS).astype(BF16)
    steps = jnp.arange(SIDE, dtype=jnp.int32)
    block_ids = ((inner // SIDE + steps) % SIDE)[:, None] * SIDE + (inner + steps) % SIDE
    block_ids = block_ids.reshape(-1)
    turned = turned_context(block_ids, context)
    w_t = w_out.T
    back_table = jnp.concatenate([token_table, token_table], 1).reshape(1, -1)
    place = jnp.stack([x, core])
    returned, grad_down, grad_gate, grad_up, turned, w_t, back_table, place = (
        lax.optimization_barrier(
            (returned, grad_down, grad_gate, grad_up, turned, w_t, back_table, place)
        )
    )
    returned = returned.reshape(devices * 2 * most, half)

    own = sum_back(back_table, returned, out_grad)

    def step(blocks, count, z_path):
        out = []
        for p in range(2):
            out.append(ahead(blocks[p], count, p == z_path))
        return out

    near = step(own, 1, 1)
    last = step(own, 3, 1)
    far = step(own, 2, 1)
    top = join(own[0], near[0], own[1], near[1])
    top_3 = step(top, 3, 0)
    top_1 = step(top, 1, 0)
    low = join(far[0], last[0], far[1], last[1])
    low_1 = step(low, 1, 0)
    low_3 = step(low, 3, 0)
    top_2 = step(top_3, 3, 0)
    low_2 = step(low_1, 1, 0)
    early = [[top[p], low[p], top_1[p], top_3[p]] for p in range(2)]
    proj_sum, ctx_sum = projected(EARLY, turned, early, w_t=w_t)
    mid = [[low_1[p], low_3[p]] for p in range(2)]
    mid, proj_sum, ctx_sum = lax.optimization_barrier((mid, proj_sum, ctx_sum))
    (proj_sum,) = projected(MID, turned, mid, before=proj_sum)
    late = [[top_2[p], low_2[p]] for p in range(2)]
    late, proj_sum = lax.optimization_barrier((late, proj_sum))
    keep, send = projected(LATE, turned, late, before=proj_sum, twin=True)
    got = lax.ppermute(send, "grp", core_pairs())
    own_share, *ahead_shares = pair_sum(place, keep, got)
    shares = [lax.ppermute(ahead_shares[k], "grp", x_pairs(k + 1)) for k in range(3)]
    rest = [[mid[p][0], late[p][0], late[p][1], mid[p][1]] for p in range(2)]
    grad_ctx = ctx_rest((3, 4, 5, 7), block_ids, ctx_sum, w_t, rest)
    proj_share = (own_share + sum(share.astype(F32) for share in shares)).astype(BF16)
    return (grad_gate[None], grad_up[None], grad_down[None], grad_ctx, proj_share)


def solution(mesh):
    rows = P(("grp", "inner"), None)
    expert = P(("grp", "inner"), None, None)
    return jax.shard_map(
        body,
        mesh=mesh,
        in_specs=(
            rows,
            rows,
            P("grp", "inner"),
            rows,
            P(),
            expert,
            expert,
            expert,
            P("inner", None),
        ),
        out_specs=(expert, expert, expert, P("grp", "inner"), P("inner", "grp")),
        check_vma=False,
    )
```

profile of v0, /device:TPU:1, one launch (start us, length us, event | category | flops | bytes accessed | tf_op | source)
XLA Modules:
  0.0 214.6 jit_solution(2006370802842255398)
XLA Ops:
  0.6 5.3 %shard_map.128 = (bf16[1024,2048]{1,0:T(8,128)(2,1)}, f32[128,128]{1,0:T(8,128)}) custom-call(s32[1]{0:T(128)} %bitcast.9.device, s32[128,256]{1,0:T(8,128)} %selected.1, bf16[128,2048]{1,0:T(8,128)(2,1)} %moe_input.1, bf16[128,2048]{1,0:T(8,128)(2,1)} %own.1), custom_call_target="tpu_custom_call" | custom-call | flops 1073741824 | bytes 5242880 | tf_op jit(solution)/shard_map/pallas_call | solution.py:92
  6.0 11.9 %all-to-all-start = ((bf16[128,8,2048]{2,1,0:T(8,128)(2,1)}), bf16[128,8,2048]{2,1,0:T(8,128)(2,1)}, u32[]{:S(2)}, u32[]{:S(2)}) async-start(bf16[128,8,2048]{2,1,0:T(8,128)(2,1)} %bitcast.38), calls=%async_computation | async-start | bytes 8388608 | tf_op jit(solution)/shard_map/all_to_all | solution.py:494
  20.4 48.2 %all-to-all-done = bf16[128,8,2048]{2,1,0:T(8,128)(2,1)} async-done(((bf16[128,8,2048]{2,1,0:T(8,128)(2,1)}), bf16[128,8,2048]{2,1,0:T(8,128)(2,1)}, u32[]{:S(2)}, u32[]{:S(2)}) %all-to-all-start) | async-done | bytes 4194336 | tf_op jit(solution)/shard_map/all_to_all | solution.py:494
  68.6 12.7 %shard_map.129 = (bf16[256,2048]{1,0:T(8,128)(2,1)}, bf16[256,2048]{1,0:T(8,128)(2,1)}, bf16[256,768]{1,0:T(8,128)(2,1)}, bf16[256,768]{1,0:T(8,128)(2,1)}, bf16...) custom-call(s32[256,1]{1,0:T(8,128)} %copy.33.position, f32[256,1]{1,0:T(8,128)} %copy.34.scale, s32[1,512]{1,0:T(1,128)} %fusion.2.spots, ...), custom_call_target="tpu_custom_call" | custom-call | flops 7247757312 | bytes 13631488 | tf_op jit(solution)/shard_map/pallas_call | solution.py:208
  81.4 6.5 %all-to-all-start.1 = ((bf16[128,8,1024]{2,1,0:T(8,128)(2,1)}), bf16[128,8,1024]{2,1,0:T(8,128)(2,1)}, u32[]{:S(2)}, u32[]{:S(2)}) async-start(bf16[128,8,1024]{2,1,0:T(8,128)(2,1)} %bitcast.39), calls=%async_computation.1 | async-start | bytes 4194304 | tf_op jit(solution)/shard_map/all_to_all | solution.py:519
  90.2 2.7 %shard_map.130 = (bf16[256,2048]{1,0:T(8,128)(2,1)S(1)}, bf16[256,2048]{1,0:T(8,128)(2,1)S(1)}) custom-call(s32[16]{0:T(128)S(1)} %add.124.table.refs_0_, bf16[2048,256]{1,0:T(8,128)(2,1)S(1)} %copy-done), custom_call_target="tpu_custom_call" | custom-call | bytes 3145728 | tf_op jit(solution)/shard_map/pallas_call | solution.py:315
  93.0 4.0 %convolution_convert_fusion.1 = bf16[2048,768]{1,0:T(8,128)(2,1)} fusion(bf16[256,2048]{1,0:T(8,128)(2,1)} %get-tuple-element.53, bf16[256,768]{1,0:T(8,128)(2,1)S(1)} %copy-done.8), kind=kOutput, calls=%fused_computation.1 | convolution fusion | flops 806879232 | bytes 4587520 | tf_op jit(solution)/shard_map/dot_general | solution.py:17
  97.1 2.7 %convolution_convert_fusion = bf16[2048,768]{1,0:T(8,128)(2,1)} fusion(bf16[256,2048]{1,0:T(8,128)(2,1)S(1)} %copy-done.2, bf16[256,768]{1,0:T(8,128)(2,1)S(1)} %copy-done.7), kind=kOutput, calls=%fused_computation | convolution fusion | flops 806879232 | bytes 4587520 | tf_op jit(solution)/shard_map/dot_general | solution.py:17
  99.8 2.7 %convolution_convert_fusion.2 = bf16[768,2048]{1,0:T(8,128)(2,1)} fusion(bf16[256,768]{1,0:T(8,128)(2,1)S(1)} %copy-done.3, bf16[256,2048]{1,0:T(8,128)(2,1)S(1)} %copy-done.5), kind=kOutput, calls=%fused_computation.2 | convolution fusion | flops 806879232 | bytes 4587520 | tf_op jit(solution)/shard_map/dot_general | solution.py:17
  102.5 14.5 %all-to-all-done.1 = bf16[128,8,1024]{2,1,0:T(8,128)(2,1)} async-done(((bf16[128,8,1024]{2,1,0:T(8,128)(2,1)}), bf16[128,8,1024]{2,1,0:T(8,128)(2,1)}, u32[]{:S(2)}, u32[]{:S(2)}) %all-to-all-start.1) | async-done | bytes 2097184 | tf_op jit(solution)/shard_map/all_to_all | solution.py:519
  123.7 4.6 %collective-permute-done.a0 = bf16[128,1024]{1,0:T(8,128)(2,1)S(1)} collective-permute-done((bf16[128,1024]{1,0:T(8,128)(2,1)S(1)}, bf16[128,1024]{1,0:T(8,128)(2,1)S(1)}, u32[]{:S(2)}, u32[]{:S(2)}) %collective-permute-start) | collective-permute-done | bytes 262176 | tf_op jit(solution)/shard_map/ppermute | solution.py:38
  128.3 7.5 %collective-permute-done.1.a1 = bf16[128,1024]{1,0:T(8,128)(2,1)S(1)} collective-permute-done((bf16[128,1024]{1,0:T(8,128)(2,1)S(1)}, bf16[128,1024]{1,0:T(8,128)(2,1)S(1)}, u32[]{:S(2)}, u32[]{:S(2)}) %collective-permute-start.1) | collective-permute-done | bytes 262176 | tf_op jit(solution)/shard_map/ppermute | solution.py:38
  143.7 3.1 %collective-permute-done.8.a1 = bf16[128,1024]{1,0:T(8,128)(2,1)S(1)} collective-permute-done((bf16[128,1024]{1,0:T(8,128)(2,1)S(1)}, bf16[128,1024]{1,0:T(8,128)(2,1)S(1)}, u32[]{:S(2)}, u32[]{:S(2)}) %collective-permute-start.8) | collective-permute-done | bytes 262176 | tf_op jit(solution)/shard_map/ppermute | solution.py:38
  146.8 10.0 %collective-permute-done.9.b1 = bf16[128,1024]{1,0:T(8,128)(2,1)S(1)} collective-permute-done((bf16[128,1024]{1,0:T(8,128)(2,1)S(1)}, bf16[128,1024]{1,0:T(8,128)(2,1)S(1)}, u32[]{:S(2)}, u32[]{:S(2)}) %collective-permute-start.9) | collective-permute-done | bytes 262176 | tf_op jit(solution)/shard_map/ppermute | solution.py:38
  156.9 2.7 %collective-permute-start.10 = (bf16[256,1024]{1,0:T(8,128)(2,1)S(1)}, bf16[256,1024]{1,0:T(8,128)(2,1)S(1)}, u32[]{:S(2)}, u32[]{:S(2)}) collective-permute-start(bf16[256,1024]{1,0:T(8,128)(2,1)S(1)} %get-tuple-element.70.refs_8_), channel_id=1, source_target_pairs={{0,12},{1,13},{2,14},{3,15},{4,0},{5,1},{6,2},{7,3},{8,4},{9,5},{1... | collective-permute-start | bytes 1572872 | tf_op jit(solution)/shard_map/ppermute | solution.py:38
  162.3 7.8 %collective-permute-done.11.refs_11_ = bf16[256,1024]{1,0:T(8,128)(2,1)S(1)} collective-permute-done((bf16[256,1024]{1,0:T(8,128)(2,1)S(1)}, bf16[256,1024]{1,0:T(8,128)(2,1)S(1)}, u32[]{:S(2)}, u32[]{:S(2)}) %collective-permute-start.11) | collective-permute-done | bytes 524320 | tf_op jit(solution)/shard_map/ppermute | solution.py:38
  170.1 2.7 %collective-permute-start.15 = (bf16[256,1024]{1,0:T(8,128)(2,1)S(1)}, bf16[256,1024]{1,0:T(8,128)(2,1)S(1)}, u32[]{:S(2)}, u32[]{:S(2)}) collective-permute-start(bf16[256,1024]{1,0:T(8,128)(2,1)S(1)} %collective-permute-done.4.refs_4_.refs_3_), channel_id=1, source_target_pairs={{0,12},{1,13},{2,14},{3,15},{4,0},{5,1},{6,2},{7,3},{8,4},{9,5},{1... | collective-permute-start | bytes 1572872 | tf_op jit(solution)/shard_map/ppermute | solution.py:38
  173.4 2.4 %collective-permute-start.17 = (bf16[256,1024]{1,0:T(8,128)(2,1)S(1)}, bf16[256,1024]{1,0:T(8,128)(2,1)S(1)}, u32[]{:S(2)}, u32[]{:S(2)}) collective-permute-start(bf16[256,1024]{1,0:T(8,128)(2,1)S(1)} %collective-permute-done.6.refs_6_.refs_7_), channel_id=1, source_target_pairs={{0,3},{1,0},{2,1},{3,2},{4,7},{5,4},{6,5},{7,6},{8,11},{9,8},{10,9... | collective-permute-start | bytes 1572872 | tf_op jit(solution)/shard_map/ppermute | solution.py:38
  175.8 4.2 %shard_map.134 = (f32[2,4,256,256]{3,2,1,0:T(8,128)S(1)}, f32[2048,256]{1,0:T(8,128)S(1)}) custom-call(bf16[256,2048]{1,0:T(8,128)(2,1)S(1)} %get-tuple-element.68.refs_0_.refs_1_.refs_2_.refs_3_, bf16[256,2048]{1,0:T(8,128)(2,1)S(1)} %get-tuple-element.68.refs_0_.refs_1_.refs_2_.refs_3_, ...), custom_call_target="tpu_custom_call" | custom-call | flops 2147483648 | bytes 6291456 | tf_op jit(solution)/shard_map/pallas_call | solution.py:405
  180.0 3.4 %collective-permute-done.7.refs_7_.refs_10_ = bf16[256,1024]{1,0:T(8,128)(2,1)S(1)} collective-permute-done((bf16[256,1024]{1,0:T(8,128)(2,1)S(1)}, bf16[256,1024]{1,0:T(8,128)(2,1)S(1)}, u32[]{:S(2)}, u32[]{:S(2)}) %collective-permute-start.7) | collective-permute-done | bytes 524320 | tf_op jit(solution)/shard_map/ppermute | solution.py:38
  185.4 9.2 %collective-permute-done.16.refs_8_.refs_6_ = bf16[256,1024]{1,0:T(8,128)(2,1)S(1)} collective-permute-done((bf16[256,1024]{1,0:T(8,128)(2,1)S(1)}, bf16[256,1024]{1,0:T(8,128)(2,1)S(1)}, u32[]{:S(2)}, u32[]{:S(2)}) %collective-permute-start.16) | collective-permute-done | bytes 524320 | tf_op jit(solution)/shard_map/ppermute | solution.py:38
  196.7 3.0 %collective-permute-start.18 = (bf16[2,4,256,256]{3,2,1,0:T(8,128)(2,1)S(1)}, bf16[2,4,256,256]{3,2,1,0:T(8,128)(2,1)S(1)}, u32[]{:S(2)}, u32[]{:S(2)}) collective-permute-start(bf16[2,4,256,256]{3,2,1,0:T(8,128)(2,1)S(1)} %get-tuple-element.88), channel_id=1, source_target_pairs={{0,16},{16,0},{32,48},{48,32},{64,80},{80,64},{96,112},{112,96},{1... | collective-permute-start | bytes 3145736 | tf_op jit(solution)/shard_map/ppermute | solution.py:565
  204.9 2.9 %shard_map.136 = bf16[2048,256]{1,0:T(8,128)(2,1)} custom-call(s32[16]{0:T(128)S(1)} %add.124.table.refs_0_, f32[2048,256]{1,0:T(8,128)S(1)} %get-tuple-element.75.refs_1_, bf16[2048,256]{1,0:T(8,128)(2,1)S(1)} %bitcast.34, bf16[256,1024]{1,0:T(8,128)(2,1)S(1)} %collective-permute-done.4.refs_4_.refs_3_, ...), custom_call_target="tpu_custom_call" | custom-call | flops 1073741824 | bytes 4194304 | tf_op jit(solution)/shard_map/pallas_call | solution.py:469
  210.0 3.8 %collective-permute-done.19 = bf16[256,256]{1,0:T(8,128)(2,1)S(1)} collective-permute-done((bf16[256,256]{1,0:T(8,128)(2,1)S(1)}, bf16[256,256]{1,0:T(8,128)(2,1)S(1)}, u32[]{:S(2)}, u32[]{:S(2)}) %collective-permute-start.19) | collective-permute-done | bytes 131104 | tf_op jit(solution)/shard_map/ppermute | solution.py:567
  (82 shorter events, 35.0 us)
Async XLA Ops:
  6.0 62.7 %all-to-all-start = ((bf16[128,8,2048]{2,1,0:T(8,128)(2,1)}), bf16[128,8,2048]{2,1,0:T(8,128)(2,1)}, u32[]{:S(2)}, u32[]{:S(2)}) async-start(bf16[128,8,2048]{2,1,0:T(8,128)(2,1)} %bitcast.38), calls=%async_computation | async-start | bytes 8388608 | tf_op jit(solution)/shard_map/all_to_all | solution.py:494
  81.4 35.6 %all-to-all-start.1 = ((bf16[128,8,1024]{2,1,0:T(8,128)(2,1)}), bf16[128,8,1024]{2,1,0:T(8,128)(2,1)}, u32[]{:S(2)}, u32[]{:S(2)}) async-start(bf16[128,8,1024]{2,1,0:T(8,128)(2,1)} %bitcast.39), calls=%async_computation.1 | async-start | bytes 4194304 | tf_op jit(solution)/shard_map/all_to_all | solution.py:519
  120.3 8.0 %collective-permute-start = (bf16[128,1024]{1,0:T(8,128)(2,1)S(1)}, bf16[128,1024]{1,0:T(8,128)(2,1)S(1)}, u32[]{:S(2)}, u32[]{:S(2)}) collective-permute-start(bf16[128,1024]{1,0:T(8,128)(2,1)S(1)} %get-tuple-element.64.a0), channel_id=1, source_target_pairs={{0,2},{1,3},{2,0},{3,1},{4,6},{5,7},{6,4},{7,5},{8,10},{9,11},{10,... | collective-permute-start | bytes 786440 | tf_op jit(solution)/shard_map/ppermute | solution.py:38
  122.5 13.3 %collective-permute-start.1 = (bf16[128,1024]{1,0:T(8,128)(2,1)S(1)}, bf16[128,1024]{1,0:T(8,128)(2,1)S(1)}, u32[]{:S(2)}, u32[]{:S(2)}) collective-permute-start(bf16[128,1024]{1,0:T(8,128)(2,1)S(1)} %get-tuple-element.64.a0), channel_id=1, source_target_pairs={{0,1},{1,2},{2,3},{3,0},{4,5},{5,6},{6,7},{7,4},{8,9},{9,10},{10,1... | collective-permute-start | bytes 786440 | tf_op jit(solution)/shard_map/ppermute | solution.py:38
  123.2 12.5 %collective-permute-start.2 = (bf16[128,1024]{1,0:T(8,128)(2,1)S(1)}, bf16[128,1024]{1,0:T(8,128)(2,1)S(1)}, u32[]{:S(2)}, u32[]{:S(2)}) collective-permute-start(bf16[128,1024]{1,0:T(8,128)(2,1)S(1)} %get-tuple-element.65.b0), channel_id=1, source_target_pairs={{0,8},{1,9},{2,10},{3,11},{4,12},{5,13},{6,14},{7,15},{8,0},{9,1},... | collective-permute-start | bytes 786440 | tf_op jit(solution)/shard_map/ppermute | solution.py:38
  123.3 14.9 %collective-permute-start.3 = (bf16[128,1024]{1,0:T(8,128)(2,1)S(1)}, bf16[128,1024]{1,0:T(8,128)(2,1)S(1)}, u32[]{:S(2)}, u32[]{:S(2)}) collective-permute-start(bf16[128,1024]{1,0:T(8,128)(2,1)S(1)} %get-tuple-element.65.b0), channel_id=1, source_target_pairs={{0,4},{1,5},{2,6},{3,7},{4,8},{5,9},{6,10},{7,11},{8,12},{9,13},{1... | collective-permute-start | bytes 786440 | tf_op jit(solution)/shard_map/ppermute | solution.py:38
  138.3 21.3 %collective-permute-start.4 = (bf16[256,1024]{1,0:T(8,128)(2,1)S(1)}, bf16[256,1024]{1,0:T(8,128)(2,1)S(1)}, u32[]{:S(2)}, u32[]{:S(2)}) collective-permute-start(bf16[256,1024]{1,0:T(8,128)(2,1)S(1)} %get-tuple-element.66.refs_9_), channel_id=1, source_target_pairs={{0,12},{1,13},{2,14},{3,15},{4,0},{5,1},{6,2},{7,3},{8,4},{9,5},{1... | collective-permute-start | bytes 1572872 | tf_op jit(solution)/shard_map/ppermute | solution.py:38
  138.4 21.7 %collective-permute-start.5 = (bf16[256,1024]{1,0:T(8,128)(2,1)S(1)}, bf16[256,1024]{1,0:T(8,128)(2,1)S(1)}, u32[]{:S(2)}, u32[]{:S(2)}) collective-permute-start(bf16[256,1024]{1,0:T(8,128)(2,1)S(1)} %get-tuple-element.66.refs_9_), channel_id=1, source_target_pairs={{0,4},{1,5},{2,6},{3,7},{4,8},{5,9},{6,10},{7,11},{8,12},{9,13},{1... | collective-permute-start | bytes 1572872 | tf_op jit(solution)/shard_map/ppermute | solution.py:38
  139.8 7.0 %collective-permute-start.8 = (bf16[128,1024]{1,0:T(8,128)(2,1)S(1)}, bf16[128,1024]{1,0:T(8,128)(2,1)S(1)}, u32[]{:S(2)}, u32[]{:S(2)}) collective-permute-start(bf16[128,1024]{1,0:T(8,128)(2,1)S(1)} %get-tuple-element.64.a0), channel_id=1, source_target_pairs={{0,3},{1,0},{2,1},{3,2},{4,7},{5,4},{6,5},{7,6},{8,11},{9,8},{10,9... | collective-permute-start | bytes 786440 | tf_op jit(solution)/shard_map/ppermute | solution.py:38
  142.2 14.6 %collective-permute-start.9 = (bf16[128,1024]{1,0:T(8,128)(2,1)S(1)}, bf16[128,1024]{1,0:T(8,128)(2,1)S(1)}, u32[]{:S(2)}, u32[]{:S(2)}) collective-permute-start(bf16[128,1024]{1,0:T(8,128)(2,1)S(1)} %get-tuple-element.65.b0), channel_id=1, source_target_pairs={{0,12},{1,13},{2,14},{3,15},{4,0},{5,1},{6,2},{7,3},{8,4},{9,5},{1... | collective-permute-start | bytes 786440 | tf_op jit(solution)/shard_map/ppermute | solution.py:38
  143.5 18.8 %collective-permute-start.6 = (bf16[256,1024]{1,0:T(8,128)(2,1)S(1)}, bf16[256,1024]{1,0:T(8,128)(2,1)S(1)}, u32[]{:S(2)}, u32[]{:S(2)}) collective-permute-start(bf16[256,1024]{1,0:T(8,128)(2,1)S(1)} %get-tuple-element.67.refs_13_), channel_id=1, source_target_pairs={{0,3},{1,0},{2,1},{3,2},{4,7},{5,4},{6,5},{7,6},{8,11},{9,8},{10,9... | collective-permute-start | bytes 1572872 | tf_op jit(solution)/shard_map/ppermute | solution.py:38
  156.8 13.2 %collective-permute-start.11 = (bf16[256,1024]{1,0:T(8,128)(2,1)S(1)}, bf16[256,1024]{1,0:T(8,128)(2,1)S(1)}, u32[]{:S(2)}, u32[]{:S(2)}) collective-permute-start(bf16[256,1024]{1,0:T(8,128)(2,1)S(1)} %get-tuple-element.70.refs_8_), channel_id=1, source_target_pairs={{0,4},{1,5},{2,6},{3,7},{4,8},{5,9},{6,10},{7,11},{8,12},{9,13},{1... | collective-permute-start | bytes 1572872 | tf_op jit(solution)/shard_map/ppermute | solution.py:38
  156.9 13.1 %collective-permute-start.10 = (bf16[256,1024]{1,0:T(8,128)(2,1)S(1)}, bf16[256,1024]{1,0:T(8,128)(2,1)S(1)}, u32[]{:S(2)}, u32[]{:S(2)}) collective-permute-start(bf16[256,1024]{1,0:T(8,128)(2,1)S(1)} %get-tuple-element.70.refs_8_), channel_id=1, source_target_pairs={{0,12},{1,13},{2,14},{3,15},{4,0},{5,1},{6,2},{7,3},{8,4},{9,5},{1... | collective-permute-start | bytes 1572872 | tf_op jit(solution)/shard_map/ppermute | solution.py:38
  159.6 13.2 %collective-permute-start.13 = (bf16[256,1024]{1,0:T(8,128)(2,1)S(1)}, bf16[256,1024]{1,0:T(8,128)(2,1)S(1)}, u32[]{:S(2)}, u32[]{:S(2)}) collective-permute-start(bf16[256,1024]{1,0:T(8,128)(2,1)S(1)} %get-tuple-element.71.refs_12_), channel_id=1, source_target_pairs={{0,1},{1,2},{2,3},{3,0},{4,5},{5,6},{6,7},{7,4},{8,9},{9,10},{10,1... | collective-permute-start | bytes 1572872 | tf_op jit(solution)/shard_map/ppermute | solution.py:38
  160.1 13.3 %collective-permute-start.12 = (bf16[256,1024]{1,0:T(8,128)(2,1)S(1)}, bf16[256,1024]{1,0:T(8,128)(2,1)S(1)}, u32[]{:S(2)}, u32[]{:S(2)}) collective-permute-start(bf16[256,1024]{1,0:T(8,128)(2,1)S(1)} %get-tuple-element.71.refs_12_), channel_id=1, source_target_pairs={{0,3},{1,0},{2,1},{3,2},{4,7},{5,4},{6,5},{7,6},{8,11},{9,8},{10,9... | collective-permute-start | bytes 1572872 | tf_op jit(solution)/shard_map/ppermute | solution.py:38
  162.3 21.1 %collective-permute-start.7 = (bf16[256,1024]{1,0:T(8,128)(2,1)S(1)}, bf16[256,1024]{1,0:T(8,128)(2,1)S(1)}, u32[]{:S(2)}, u32[]{:S(2)}) collective-permute-start(bf16[256,1024]{1,0:T(8,128)(2,1)S(1)} %get-tuple-element.67.refs_13_), channel_id=1, source_target_pairs={{0,1},{1,2},{2,3},{3,0},{4,5},{5,6},{6,7},{7,4},{8,9},{9,10},{10,1... | collective-permute-start | bytes 1572872 | tf_op jit(solution)/shard_map/ppermute | solution.py:38
  170.0 15.3 %collective-permute-start.14 = (bf16[256,1024]{1,0:T(8,128)(2,1)S(1)}, bf16[256,1024]{1,0:T(8,128)(2,1)S(1)}, u32[]{:S(2)}, u32[]{:S(2)}) collective-permute-start(bf16[256,1024]{1,0:T(8,128)(2,1)S(1)} %collective-permute-done.11.refs_11_), channel_id=1, source_target_pairs={{0,4},{1,5},{2,6},{3,7},{4,8},{5,9},{6,10},{7,11},{8,12},{9,13},{1... | collective-permute-start | bytes 1572872 | tf_op jit(solution)/shard_map/ppermute | solution.py:38
  170.1 15.3 %collective-permute-start.15 = (bf16[256,1024]{1,0:T(8,128)(2,1)S(1)}, bf16[256,1024]{1,0:T(8,128)(2,1)S(1)}, u32[]{:S(2)}, u32[]{:S(2)}) collective-permute-start(bf16[256,1024]{1,0:T(8,128)(2,1)S(1)} %collective-permute-done.4.refs_4_.refs_3_), channel_id=1, source_target_pairs={{0,12},{1,13},{2,14},{3,15},{4,0},{5,1},{6,2},{7,3},{8,4},{9,5},{1... | collective-permute-start | bytes 1572872 | tf_op jit(solution)/shard_map/ppermute | solution.py:38
  172.7 21.9 %collective-permute-start.16 = (bf16[256,1024]{1,0:T(8,128)(2,1)S(1)}, bf16[256,1024]{1,0:T(8,128)(2,1)S(1)}, u32[]{:S(2)}, u32[]{:S(2)}) collective-permute-start(bf16[256,1024]{1,0:T(8,128)(2,1)S(1)} %collective-permute-done.13.refs_15_), channel_id=1, source_target_pairs={{0,1},{1,2},{2,3},{3,0},{4,5},{5,6},{6,7},{7,4},{8,9},{9,10},{10,1... | collective-permute-start | bytes 1572872 | tf_op jit(solution)/shard_map/ppermute | solution.py:38
  173.4 21.3 %collective-permute-start.17 = (bf16[256,1024]{1,0:T(8,128)(2,1)S(1)}, bf16[256,1024]{1,0:T(8,128)(2,1)S(1)}, u32[]{:S(2)}, u32[]{:S(2)}) collective-permute-start(bf16[256,1024]{1,0:T(8,128)(2,1)S(1)} %collective-permute-done.6.refs_6_.refs_7_), channel_id=1, source_target_pairs={{0,3},{1,0},{2,1},{3,2},{4,7},{5,4},{6,5},{7,6},{8,11},{9,8},{10,9... | collective-permute-start | bytes 1572872 | tf_op jit(solution)/shard_map/ppermute | solution.py:38
  196.7 5.3 %collective-permute-start.18 = (bf16[2,4,256,256]{3,2,1,0:T(8,128)(2,1)S(1)}, bf16[2,4,256,256]{3,2,1,0:T(8,128)(2,1)S(1)}, u32[]{:S(2)}, u32[]{:S(2)}) collective-permute-start(bf16[2,4,256,256]{3,2,1,0:T(8,128)(2,1)S(1)} %get-tuple-element.88), channel_id=1, source_target_pairs={{0,16},{16,0},{32,48},{48,32},{64,80},{80,64},{96,112},{112,96},{1... | collective-permute-start | bytes 3145736 | tf_op jit(solution)/shard_map/ppermute | solution.py:565
  202.7 5.0 %collective-permute-start.21 = (bf16[256,256]{1,0:T(8,128)(2,1)S(1)}, bf16[256,256]{1,0:T(8,128)(2,1)S(1)}, u32[]{:S(2)}, u32[]{:S(2)}) collective-permute-start(bf16[256,256]{1,0:T(8,128)(2,1)S(1)} %get-tuple-element.92), channel_id=1, source_target_pairs={{0,96},{16,112},{32,0},{48,16},{64,32},{80,48},{96,64},{112,80},{1... | collective-permute-start | bytes 393224 | tf_op jit(solution)/shard_map/ppermute | solution.py:567
  204.1 5.9 %collective-permute-start.20 = (bf16[256,256]{1,0:T(8,128)(2,1)S(1)}, bf16[256,256]{1,0:T(8,128)(2,1)S(1)}, u32[]{:S(2)}, u32[]{:S(2)}) collective-permute-start(bf16[256,256]{1,0:T(8,128)(2,1)S(1)} %get-tuple-element.91), channel_id=1, source_target_pairs={{0,64},{16,80},{32,96},{48,112},{64,0},{80,16},{96,32},{112,48},{1... | collective-permute-start | bytes 393224 | tf_op jit(solution)/shard_map/ppermute | solution.py:567
  204.7 9.2 %collective-permute-start.19 = (bf16[256,256]{1,0:T(8,128)(2,1)S(1)}, bf16[256,256]{1,0:T(8,128)(2,1)S(1)}, u32[]{:S(2)}, u32[]{:S(2)}) collective-permute-start(bf16[256,256]{1,0:T(8,128)(2,1)S(1)} %get-tuple-element.90), channel_id=1, source_target_pairs={{0,32},{16,48},{32,64},{48,80},{64,96},{80,112},{96,0},{112,16},{1... | collective-permute-start | bytes 393224 | tf_op jit(solution)/shard_map/ppermute | solution.py:567
  (11 other events, 66.5 us)
where the time goes:
time: 215 us
  waiting for transfers between devices  119 us (55%)
  starting transfers between devices  43.6 us (20%)
  Pallas kernels  34.9 us (16%)
  matrix products  9.43 us (4%)
  local copies, waits for them, and re-layouts  4.79 us (2%)
    all_to_all x1, waiting for transfers between devices, body(): lax.all_to_all(sent.reshape(devices, 2 * most, width), both, split_axis=0...  48.2 us
    ppermute x18, waiting for transfers between devices, ahead(): return lax.ppermute(block, 'inner', ring_pairs(-step, along_z))  48.1 us
    ppermute x18, starting transfers between devices, ahead(): return lax.ppermute(block, 'inner', ring_pairs(-step, along_z))  19.9 us
    all_to_all x1, waiting for transfers between devices, body(): lax.all_to_all(placed, both, split_axis=0, concat_axis=0, tiled=True)  14.5 us
    pallas_call x1, Pallas kernels, expert(): pl.pallas_call(expert_kernel, out_shape=[jax.ShapeDtypeStruct(shape, BF16...  12.7 us
    all_to_all x1, starting transfers between devices, body(): lax.all_to_all(sent.reshape(devices, 2 * most, width), both, split_axis=0...  11.9 us
    dot_general x3, matrix products, dot(): return lax.dot_general(left, right, dims, preferred_element_type=F32)  9.43 us
    pallas_call x3, Pallas kernels, projected(): pl.pallas_call(lambda *refs: proj_kernel(spots, w_t is not None, before i...  8.2 us
  transfers between devices with their start and end apart: 24, of which 13 were waited for; matrix products, arithmetic and copies ran while one was open for 6% of the time, Pallas kernels for 5%

commit v1 on v0

--- a/solution.py
+++ b/solution.py
@@ -135,8 +135,7 @@
     def store(n, source):
         return pltpu.make_async_copy(source, results[n], out_sem.at[n])
 
-    ahead_by = 2
-    for k in range(ahead_by):
+    for k in range(count):
         for copy in fetches(k):
             copy.start()
     spot = lax.broadcasted_iota(jnp.int32, (slots, depth), 1)
@@ -153,9 +152,6 @@
         scaled_in[:, cols] = scaled
         for copy in waits[1:]:
             copy.wait()
-        if k + ahead_by < count:
-            for copy in fetches(k + ahead_by):
-                copy.start()
         terms = (
             (gate_sum, dot(rows, gate_w[cols, :])),
             (up_sum, dot(rows, up_w[cols, :])),
@@ -278,7 +274,7 @@
             pltpu.VMEM(own.shape, BF16),
             pltpu.SemaphoreType.DMA((count + 1,)),
         ],
-        compiler_params=small(16),
+        compiler_params=small(59),
         cost_estimate=cost(4 * tokens * rows * cols, 2 * rows * cols),
     )(table, back, own)
 

time: 215 us -> 218 us (1.014)
  Pallas kernels: 34.9 us -> 37.1 us
where the time goes in v1:
time: 218 us
  waiting for transfers between devices  119 us (55%)
  starting transfers between devices  43.2 us (20%)
  Pallas kernels  37.1 us (17%)
  matrix products  9.42 us (4%)
  local copies, waits for them, and re-layouts  6.25 us (3%)
    ppermute x18, waiting for transfers between devices, ahead(): return lax.ppermute(block, 'inner', ring_pairs(-step, along_z))  48.6 us
    all_to_all x1, waiting for transfers between devices, body(): lax.all_to_all(sent.reshape(devices, 2 * most, width), both, split_axis=0...  48.2 us
    ppermute x18, starting transfers between devices, ahead(): return lax.ppermute(block, 'inner', ring_pairs(-step, along_z))  19.7 us
    all_to_all x1, waiting for transfers between devices, body(): lax.all_to_all(placed, both, split_axis=0, concat_axis=0, tiled=True)  13.9 us
    pallas_call x1, Pallas kernels, expert(): pl.pallas_call(expert_kernel, out_shape=[jax.ShapeDtypeStruct(shape, BF16...  12.7 us
    all_to_all x1, starting transfers between devices, body(): lax.all_to_all(sent.reshape(devices, 2 * most, width), both, split_axis=0...  11.9 us
    dot_general x3, matrix products, dot(): return lax.dot_general(left, right, dims, preferred_element_type=F32)  9.42 us
    pallas_call x3, Pallas kernels, projected(): pl.pallas_call(lambda *refs: proj_kernel(spots, w_t is not None, before i...  8.2 us
  transfers between devices with their start and end apart: 24, of which 13 were waited for; matrix products, arithmetic and copies ran while one was open for 6% of the time, Pallas kernels for 5%

profile of v1, /device:TPU:1, one launch (start us, length us, event | category | flops | bytes accessed | tf_op | source)
XLA Modules:
  0.0 217.9 jit_solution(626656890466697366)
XLA Ops:
  0.6 5.3 %shard_map.128 = (bf16[1024,2048]{1,0:T(8,128)(2,1)}, f32[128,128]{1,0:T(8,128)}) custom-call(s32[1]{0:T(128)} %bitcast.9.device, s32[128,256]{1,0:T(8,128)} %selected.1, bf16[128,2048]{1,0:T(8,128)(2,1)} %moe_input.1, bf16[128,2048]{1,0:T(8,128)(2,1)} %own.1), custom_call_target="tpu_custom_call" | custom-call | flops 1073741824 | bytes 5242880 | tf_op jit(solution)/shard_map/pallas_call | solution.py:92
  6.0 11.9 %all-to-all-start = ((bf16[128,8,2048]{2,1,0:T(8,128)(2,1)}), bf16[128,8,2048]{2,1,0:T(8,128)(2,1)}, u32[]{:S(2)}, u32[]{:S(2)}) async-start(bf16[128,8,2048]{2,1,0:T(8,128)(2,1)} %bitcast.38), calls=%async_computation | async-start | bytes 8388608 | tf_op jit(solution)/shard_map/all_to_all | solution.py:490
  20.4 48.2 %all-to-all-done = bf16[128,8,2048]{2,1,0:T(8,128)(2,1)} async-done(((bf16[128,8,2048]{2,1,0:T(8,128)(2,1)}), bf16[128,8,2048]{2,1,0:T(8,128)(2,1)}, u32[]{:S(2)}, u32[]{:S(2)}) %all-to-all-start) | async-done | bytes 4194336 | tf_op jit(solution)/shard_map/all_to_all | solution.py:490
  68.6 12.7 %shard_map.129 = (bf16[256,2048]{1,0:T(8,128)(2,1)}, bf16[256,2048]{1,0:T(8,128)(2,1)}, bf16[256,768]{1,0:T(8,128)(2,1)}, bf16[256,768]{1,0:T(8,128)(2,1)}, bf16...) custom-call(s32[256,1]{1,0:T(8,128)} %copy.33.position, f32[256,1]{1,0:T(8,128)} %copy.34.scale, s32[1,512]{1,0:T(1,128)} %fusion.2.spots, ...), custom_call_target="tpu_custom_call" | custom-call | flops 7247757312 | bytes 13631488 | tf_op jit(solution)/shard_map/pallas_call | solution.py:204
  81.4 6.5 %all-to-all-start.1 = ((bf16[128,8,1024]{2,1,0:T(8,128)(2,1)}), bf16[128,8,1024]{2,1,0:T(8,128)(2,1)}, u32[]{:S(2)}, u32[]{:S(2)}) async-start(bf16[128,8,1024]{2,1,0:T(8,128)(2,1)} %bitcast.39), calls=%async_computation.1 | async-start | bytes 4194304 | tf_op jit(solution)/shard_map/all_to_all | solution.py:515
  90.7 2.7 %shard_map.130 = (bf16[256,2048]{1,0:T(8,128)(2,1)S(1)}, bf16[256,2048]{1,0:T(8,128)(2,1)S(1)}) custom-call(s32[16]{0:T(128)S(1)} %add.124.table.refs_0_, bf16[2048,256]{1,0:T(8,128)(2,1)S(1)} %copy-done), custom_call_target="tpu_custom_call" | custom-call | bytes 3145728 | tf_op jit(solution)/shard_map/pallas_call | solution.py:311
  93.6 4.0 %convolution_convert_fusion.1 = bf16[2048,768]{1,0:T(8,128)(2,1)} fusion(bf16[256,2048]{1,0:T(8,128)(2,1)} %get-tuple-element.53, bf16[256,768]{1,0:T(8,128)(2,1)S(1)} %copy-done.9), kind=kOutput, calls=%fused_computation.1 | convolution fusion | flops 806879232 | bytes 4587520 | tf_op jit(solution)/shard_map/dot_general | solution.py:17
  97.6 2.7 %convolution_convert_fusion = bf16[2048,768]{1,0:T(8,128)(2,1)} fusion(bf16[256,2048]{1,0:T(8,128)(2,1)S(1)} %copy-done.3, bf16[256,768]{1,0:T(8,128)(2,1)S(1)} %copy-done.8), kind=kOutput, calls=%fused_computation | convolution fusion | flops 806879232 | bytes 4587520 | tf_op jit(solution)/shard_map/dot_general | solution.py:17
  100.3 2.7 %convolution_convert_fusion.2 = bf16[768,2048]{1,0:T(8,128)(2,1)} fusion(bf16[256,768]{1,0:T(8,128)(2,1)S(1)} %copy-done.4, bf16[256,2048]{1,0:T(8,128)(2,1)S(1)} %copy-done.6), kind=kOutput, calls=%fused_computation.2 | convolution fusion | flops 806879232 | bytes 4587520 | tf_op jit(solution)/shard_map/dot_general | solution.py:17
  103.0 13.9 %all-to-all-done.1 = bf16[128,8,1024]{2,1,0:T(8,128)(2,1)} async-done(((bf16[128,8,1024]{2,1,0:T(8,128)(2,1)}), bf16[128,8,1024]{2,1,0:T(8,128)(2,1)}, u32[]{:S(2)}, u32[]{:S(2)}) %all-to-all-start.1) | async-done | bytes 2097184 | tf_op jit(solution)/shard_map/all_to_all | solution.py:515
  116.9 4.5 %shard_map.131 = (bf16[128,1024]{1,0:T(8,128)(2,1)}, bf16[128,1024]{1,0:T(8,128)(2,1)}) custom-call(s32[1,1024]{1,0:T(1,128)} %reshape.143.table, bf16[1024,1024]{1,0:T(8,128)(2,1)} %bitcast.19.back, bf16[128,2048]{1,0:T(8,128)(2,1)} %own.1), custom_call_target="tpu_custom_call" | custom-call | flops 536870912 | bytes 2097152 | tf_op jit(solution)/shard_map/pallas_call | solution.py:268
  124.8 4.9 %collective-permute-done.a0 = bf16[128,1024]{1,0:T(8,128)(2,1)S(1)} collective-permute-done((bf16[128,1024]{1,0:T(8,128)(2,1)}, bf16[128,1024]{1,0:T(8,128)(2,1)S(1)}, u32[]{:S(2)}, u32[]{:S(2)}) %collective-permute-start) | collective-permute-done | bytes 262176 | tf_op jit(solution)/shard_map/ppermute | solution.py:38
  129.7 7.4 %collective-permute-done.1.a1 = bf16[128,1024]{1,0:T(8,128)(2,1)S(1)} collective-permute-done((bf16[128,1024]{1,0:T(8,128)(2,1)}, bf16[128,1024]{1,0:T(8,128)(2,1)S(1)}, u32[]{:S(2)}, u32[]{:S(2)}) %collective-permute-start.1) | collective-permute-done | bytes 262176 | tf_op jit(solution)/shard_map/ppermute | solution.py:38
  145.0 3.4 %collective-permute-done.8.a1 = bf16[128,1024]{1,0:T(8,128)(2,1)S(1)} collective-permute-done((bf16[128,1024]{1,0:T(8,128)(2,1)}, bf16[128,1024]{1,0:T(8,128)(2,1)S(1)}, u32[]{:S(2)}, u32[]{:S(2)}) %collective-permute-start.8) | collective-permute-done | bytes 262176 | tf_op jit(solution)/shard_map/ppermute | solution.py:38
  148.4 9.8 %collective-permute-done.9.b1 = bf16[128,1024]{1,0:T(8,128)(2,1)S(1)} collective-permute-done((bf16[128,1024]{1,0:T(8,128)(2,1)}, bf16[128,1024]{1,0:T(8,128)(2,1)S(1)}, u32[]{:S(2)}, u32[]{:S(2)}) %collective-permute-start.9) | collective-permute-done | bytes 262176 | tf_op jit(solution)/shard_map/ppermute | solution.py:38
  160.2 2.7 %collective-permute-start.10 = (bf16[256,1024]{1,0:T(8,128)(2,1)S(1)}, bf16[256,1024]{1,0:T(8,128)(2,1)S(1)}, u32[]{:S(2)}, u32[]{:S(2)}) collective-permute-start(bf16[256,1024]{1,0:T(8,128)(2,1)S(1)} %get-tuple-element.70.refs_8_), channel_id=1, source_target_pairs={{0,12},{1,13},{2,14},{3,15},{4,0},{5,1},{6,2},{7,3},{8,4},{9,5},{1... | collective-permute-start | bytes 1572872 | tf_op jit(solution)/shard_map/ppermute | solution.py:38
  165.6 7.8 %collective-permute-done.11.refs_11_ = bf16[256,1024]{1,0:T(8,128)(2,1)S(1)} collective-permute-done((bf16[256,1024]{1,0:T(8,128)(2,1)S(1)}, bf16[256,1024]{1,0:T(8,128)(2,1)S(1)}, u32[]{:S(2)}, u32[]{:S(2)}) %collective-permute-start.11) | collective-permute-done | bytes 524320 | tf_op jit(solution)/shard_map/ppermute | solution.py:38
  173.4 2.7 %collective-permute-start.15 = (bf16[256,1024]{1,0:T(8,128)(2,1)S(1)}, bf16[256,1024]{1,0:T(8,128)(2,1)S(1)}, u32[]{:S(2)}, u32[]{:S(2)}) collective-permute-start(bf16[256,1024]{1,0:T(8,128)(2,1)S(1)} %collective-permute-done.4.refs_4_.refs_3_), channel_id=1, source_target_pairs={{0,12},{1,13},{2,14},{3,15},{4,0},{5,1},{6,2},{7,3},{8,4},{9,5},{1... | collective-permute-start | bytes 1572872 | tf_op jit(solution)/shard_map/ppermute | solution.py:38
  179.0 4.2 %shard_map.134 = (f32[2,4,256,256]{3,2,1,0:T(8,128)S(1)}, f32[2048,256]{1,0:T(8,128)S(1)}) custom-call(bf16[256,2048]{1,0:T(8,128)(2,1)S(1)} %get-tuple-element.68.refs_0_.refs_1_.refs_2_.refs_3_, bf16[256,2048]{1,0:T(8,128)(2,1)S(1)} %get-tuple-element.68.refs_0_.refs_1_.refs_2_.refs_3_, ...), custom_call_target="tpu_custom_call" | custom-call | flops 2147483648 | bytes 6291456 | tf_op jit(solution)/shard_map/pallas_call | solution.py:401
  183.2 3.6 %collective-permute-done.7.refs_7_.refs_10_ = bf16[256,1024]{1,0:T(8,128)(2,1)S(1)} collective-permute-done((bf16[256,1024]{1,0:T(8,128)(2,1)S(1)}, bf16[256,1024]{1,0:T(8,128)(2,1)S(1)}, u32[]{:S(2)}, u32[]{:S(2)}) %collective-permute-start.7) | collective-permute-done | bytes 524320 | tf_op jit(solution)/shard_map/ppermute | solution.py:38
  188.7 9.2 %collective-permute-done.16.refs_8_.refs_6_ = bf16[256,1024]{1,0:T(8,128)(2,1)S(1)} collective-permute-done((bf16[256,1024]{1,0:T(8,128)(2,1)S(1)}, bf16[256,1024]{1,0:T(8,128)(2,1)S(1)}, u32[]{:S(2)}, u32[]{:S(2)}) %collective-permute-start.16) | collective-permute-done | bytes 524320 | tf_op jit(solution)/shard_map/ppermute | solution.py:38
  200.0 3.0 %collective-permute-start.18 = (bf16[2,4,256,256]{3,2,1,0:T(8,128)(2,1)S(1)}, bf16[2,4,256,256]{3,2,1,0:T(8,128)(2,1)S(1)}, u32[]{:S(2)}, u32[]{:S(2)}) collective-permute-start(bf16[2,4,256,256]{3,2,1,0:T(8,128)(2,1)S(1)} %get-tuple-element.88), channel_id=1, source_target_pairs={{0,16},{16,0},{32,48},{48,32},{64,80},{80,64},{96,112},{112,96},{1... | collective-permute-start | bytes 3145736 | tf_op jit(solution)/shard_map/ppermute | solution.py:561
  208.1 2.9 %shard_map.136 = bf16[2048,256]{1,0:T(8,128)(2,1)} custom-call(s32[16]{0:T(128)S(1)} %add.124.table.refs_0_, f32[2048,256]{1,0:T(8,128)S(1)} %get-tuple-element.75.refs_1_, bf16[2048,256]{1,0:T(8,128)(2,1)S(1)} %bitcast.34, bf16[256,1024]{1,0:T(8,128)(2,1)S(1)} %collective-permute-done.4.refs_4_.refs_3_, ...), custom_call_target="tpu_custom_call" | custom-call | flops 1073741824 | bytes 4194304 | tf_op jit(solution)/shard_map/pallas_call | solution.py:465
  213.3 3.8 %collective-permute-done.19 = bf16[256,256]{1,0:T(8,128)(2,1)S(1)} collective-permute-done((bf16[256,256]{1,0:T(8,128)(2,1)S(1)}, bf16[256,256]{1,0:T(8,128)(2,1)S(1)}, u32[]{:S(2)}, u32[]{:S(2)}) %collective-permute-start.19) | collective-permute-done | bytes 131104 | tf_op jit(solution)/shard_map/ppermute | solution.py:563
  (84 shorter events, 36.4 us)
Async XLA Ops:
  6.0 62.7 %all-to-all-start = ((bf16[128,8,2048]{2,1,0:T(8,128)(2,1)}), bf16[128,8,2048]{2,1,0:T(8,128)(2,1)}, u32[]{:S(2)}, u32[]{:S(2)}) async-start(bf16[128,8,2048]{2,1,0:T(8,128)(2,1)} %bitcast.38), calls=%async_computation | async-start | bytes 8388608 | tf_op jit(solution)/shard_map/all_to_all | solution.py:490
  81.4 35.5 %all-to-all-start.1 = ((bf16[128,8,1024]{2,1,0:T(8,128)(2,1)}), bf16[128,8,1024]{2,1,0:T(8,128)(2,1)}, u32[]{:S(2)}, u32[]{:S(2)}) async-start(bf16[128,8,1024]{2,1,0:T(8,128)(2,1)} %bitcast.39), calls=%async_computation.1 | async-start | bytes 4194304 | tf_op jit(solution)/shard_map/all_to_all | solution.py:515
  121.4 8.3 %collective-permute-start = (bf16[128,1024]{1,0:T(8,128)(2,1)}, bf16[128,1024]{1,0:T(8,128)(2,1)S(1)}, u32[]{:S(2)}, u32[]{:S(2)}) collective-permute-start(bf16[128,1024]{1,0:T(8,128)(2,1)} %get-tuple-element.64.a0), channel_id=1, source_target_pairs={{0,2},{1,3},{2,0},{3,1},{4,6},{5,7},{6,4},{7,5},{8,10},{9,11},{10,... | collective-permute-start | bytes 786440 | tf_op jit(solution)/shard_map/ppermute | solution.py:38
  123.6 13.5 %collective-permute-start.1 = (bf16[128,1024]{1,0:T(8,128)(2,1)}, bf16[128,1024]{1,0:T(8,128)(2,1)S(1)}, u32[]{:S(2)}, u32[]{:S(2)}) collective-permute-start(bf16[128,1024]{1,0:T(8,128)(2,1)} %get-tuple-element.64.a0), channel_id=1, source_target_pairs={{0,1},{1,2},{2,3},{3,0},{4,5},{5,6},{6,7},{7,4},{8,9},{9,10},{10,1... | collective-permute-start | bytes 786440 | tf_op jit(solution)/shard_map/ppermute | solution.py:38
  124.3 12.8 %collective-permute-start.2 = (bf16[128,1024]{1,0:T(8,128)(2,1)}, bf16[128,1024]{1,0:T(8,128)(2,1)S(1)}, u32[]{:S(2)}, u32[]{:S(2)}) collective-permute-start(bf16[128,1024]{1,0:T(8,128)(2,1)} %get-tuple-element.65.b0), channel_id=1, source_target_pairs={{0,8},{1,9},{2,10},{3,11},{4,12},{5,13},{6,14},{7,15},{8,0},{9,1},... | collective-permute-start | bytes 786440 | tf_op jit(solution)/shard_map/ppermute | solution.py:38
  124.4 15.2 %collective-permute-start.3 = (bf16[128,1024]{1,0:T(8,128)(2,1)}, bf16[128,1024]{1,0:T(8,128)(2,1)S(1)}, u32[]{:S(2)}, u32[]{:S(2)}) collective-permute-start(bf16[128,1024]{1,0:T(8,128)(2,1)} %get-tuple-element.65.b0), channel_id=1, source_target_pairs={{0,4},{1,5},{2,6},{3,7},{4,8},{5,9},{6,10},{7,11},{8,12},{9,13},{1... | collective-permute-start | bytes 786440 | tf_op jit(solution)/shard_map/ppermute | solution.py:38
  139.6 23.2 %collective-permute-start.4 = (bf16[256,1024]{1,0:T(8,128)(2,1)S(1)}, bf16[256,1024]{1,0:T(8,128)(2,1)S(1)}, u32[]{:S(2)}, u32[]{:S(2)}) collective-permute-start(bf16[256,1024]{1,0:T(8,128)(2,1)S(1)} %get-tuple-element.66.refs_9_), channel_id=1, source_target_pairs={{0,12},{1,13},{2,14},{3,15},{4,0},{5,1},{6,2},{7,3},{8,4},{9,5},{1... | collective-permute-start | bytes 1572872 | tf_op jit(solution)/shard_map/ppermute | solution.py:38
  139.7 23.5 %collective-permute-start.5 = (bf16[256,1024]{1,0:T(8,128)(2,1)S(1)}, bf16[256,1024]{1,0:T(8,128)(2,1)S(1)}, u32[]{:S(2)}, u32[]{:S(2)}) collective-permute-start(bf16[256,1024]{1,0:T(8,128)(2,1)S(1)} %get-tuple-element.66.refs_9_), channel_id=1, source_target_pairs={{0,4},{1,5},{2,6},{3,7},{4,8},{5,9},{6,10},{7,11},{8,12},{9,13},{1... | collective-permute-start | bytes 1572872 | tf_op jit(solution)/shard_map/ppermute | solution.py:38
  141.2 7.2 %collective-permute-start.8 = (bf16[128,1024]{1,0:T(8,128)(2,1)}, bf16[128,1024]{1,0:T(8,128)(2,1)S(1)}, u32[]{:S(2)}, u32[]{:S(2)}) collective-permute-start(bf16[128,1024]{1,0:T(8,128)(2,1)} %get-tuple-element.64.a0), channel_id=1, source_target_pairs={{0,3},{1,0},{2,1},{3,2},{4,7},{5,4},{6,5},{7,6},{8,11},{9,8},{10,9... | collective-permute-start | bytes 786440 | tf_op jit(solution)/shard_map/ppermute | solution.py:38
  143.5 14.7 %collective-permute-start.9 = (bf16[128,1024]{1,0:T(8,128)(2,1)}, bf16[128,1024]{1,0:T(8,128)(2,1)S(1)}, u32[]{:S(2)}, u32[]{:S(2)}) collective-permute-start(bf16[128,1024]{1,0:T(8,128)(2,1)} %get-tuple-element.65.b0), channel_id=1, source_target_pairs={{0,12},{1,13},{2,14},{3,15},{4,0},{5,1},{6,2},{7,3},{8,4},{9,5},{1... | collective-permute-start | bytes 786440 | tf_op jit(solution)/shard_map/ppermute | solution.py:38
  144.8 20.8 %collective-permute-start.6 = (bf16[256,1024]{1,0:T(8,128)(2,1)S(1)}, bf16[256,1024]{1,0:T(8,128)(2,1)S(1)}, u32[]{:S(2)}, u32[]{:S(2)}) collective-permute-start(bf16[256,1024]{1,0:T(8,128)(2,1)S(1)} %get-tuple-element.67.refs_13_), channel_id=1, source_target_pairs={{0,3},{1,0},{2,1},{3,2},{4,7},{5,4},{6,5},{7,6},{8,11},{9,8},{10,9... | collective-permute-start | bytes 1572872 | tf_op jit(solution)/shard_map/ppermute | solution.py:38
  160.1 13.2 %collective-permute-start.11 = (bf16[256,1024]{1,0:T(8,128)(2,1)S(1)}, bf16[256,1024]{1,0:T(8,128)(2,1)S(1)}, u32[]{:S(2)}, u32[]{:S(2)}) collective-permute-start(bf16[256,1024]{1,0:T(8,128)(2,1)S(1)} %get-tuple-element.70.refs_8_), channel_id=1, source_target_pairs={{0,4},{1,5},{2,6},{3,7},{4,8},{5,9},{6,10},{7,11},{8,12},{9,13},{1... | collective-permute-start | bytes 1572872 | tf_op jit(solution)/shard_map/ppermute | solution.py:38
  160.2 13.2 %collective-permute-start.10 = (bf16[256,1024]{1,0:T(8,128)(2,1)S(1)}, bf16[256,1024]{1,0:T(8,128)(2,1)S(1)}, u32[]{:S(2)}, u32[]{:S(2)}) collective-permute-start(bf16[256,1024]{1,0:T(8,128)(2,1)S(1)} %get-tuple-element.70.refs_8_), channel_id=1, source_target_pairs={{0,12},{1,13},{2,14},{3,15},{4,0},{5,1},{6,2},{7,3},{8,4},{9,5},{1... | collective-permute-start | bytes 1572872 | tf_op jit(solution)/shard_map/ppermute | solution.py:38
  162.9 13.2 %collective-permute-start.13 = (bf16[256,1024]{1,0:T(8,128)(2,1)S(1)}, bf16[256,1024]{1,0:T(8,128)(2,1)S(1)}, u32[]{:S(2)}, u32[]{:S(2)}) collective-permute-start(bf16[256,1024]{1,0:T(8,128)(2,1)S(1)} %get-tuple-element.71.refs_12_), channel_id=1, source_target_pairs={{0,1},{1,2},{2,3},{3,0},{4,5},{5,6},{6,7},{7,4},{8,9},{9,10},{10,1... | collective-permute-start | bytes 1572872 | tf_op jit(solution)/shard_map/ppermute | solution.py:38
  163.3 13.3 %collective-permute-start.12 = (bf16[256,1024]{1,0:T(8,128)(2,1)S(1)}, bf16[256,1024]{1,0:T(8,128)(2,1)S(1)}, u32[]{:S(2)}, u32[]{:S(2)}) collective-permute-start(bf16[256,1024]{1,0:T(8,128)(2,1)S(1)} %get-tuple-element.71.refs_12_), channel_id=1, source_target_pairs={{0,3},{1,0},{2,1},{3,2},{4,7},{5,4},{6,5},{7,6},{8,11},{9,8},{10,9... | collective-permute-start | bytes 1572872 | tf_op jit(solution)/shard_map/ppermute | solution.py:38
  165.6 21.2 %collective-permute-start.7 = (bf16[256,1024]{1,0:T(8,128)(2,1)S(1)}, bf16[256,1024]{1,0:T(8,128)(2,1)S(1)}, u32[]{:S(2)}, u32[]{:S(2)}) collective-permute-start(bf16[256,1024]{1,0:T(8,128)(2,1)S(1)} %get-tuple-element.67.refs_13_), channel_id=1, source_target_pairs={{0,1},{1,2},{2,3},{3,0},{4,5},{5,6},{6,7},{7,4},{8,9},{9,10},{10,1... | collective-permute-start | bytes 1572872 | tf_op jit(solution)/shard_map/ppermute | solution.py:38
  173.4 15.3 %collective-permute-start.14 = (bf16[256,1024]{1,0:T(8,128)(2,1)S(1)}, bf16[256,1024]{1,0:T(8,128)(2,1)S(1)}, u32[]{:S(2)}, u32[]{:S(2)}) collective-permute-start(bf16[256,1024]{1,0:T(8,128)(2,1)S(1)} %collective-permute-done.11.refs_11_), channel_id=1, source_target_pairs={{0,4},{1,5},{2,6},{3,7},{4,8},{5,9},{6,10},{7,11},{8,12},{9,13},{1... | collective-permute-start | bytes 1572872 | tf_op jit(solution)/shard_map/ppermute | solution.py:38
  173.4 15.3 %collective-permute-start.15 = (bf16[256,1024]{1,0:T(8,128)(2,1)S(1)}, bf16[256,1024]{1,0:T(8,128)(2,1)S(1)}, u32[]{:S(2)}, u32[]{:S(2)}) collective-permute-start(bf16[256,1024]{1,0:T(8,128)(2,1)S(1)} %collective-permute-done.4.refs_4_.refs_3_), channel_id=1, source_target_pairs={{0,12},{1,13},{2,14},{3,15},{4,0},{5,1},{6,2},{7,3},{8,4},{9,5},{1... | collective-permute-start | bytes 1572872 | tf_op jit(solution)/shard_map/ppermute | solution.py:38
  176.1 21.9 %collective-permute-start.16 = (bf16[256,1024]{1,0:T(8,128)(2,1)S(1)}, bf16[256,1024]{1,0:T(8,128)(2,1)S(1)}, u32[]{:S(2)}, u32[]{:S(2)}) collective-permute-start(bf16[256,1024]{1,0:T(8,128)(2,1)S(1)} %collective-permute-done.13.refs_15_), channel_id=1, source_target_pairs={{0,1},{1,2},{2,3},{3,0},{4,5},{5,6},{6,7},{7,4},{8,9},{9,10},{10,1... | collective-permute-start | bytes 1572872 | tf_op jit(solution)/shard_map/ppermute | solution.py:38
  176.6 21.4 %collective-permute-start.17 = (bf16[256,1024]{1,0:T(8,128)(2,1)S(1)}, bf16[256,1024]{1,0:T(8,128)(2,1)S(1)}, u32[]{:S(2)}, u32[]{:S(2)}) collective-permute-start(bf16[256,1024]{1,0:T(8,128)(2,1)S(1)} %collective-permute-done.6.refs_6_.refs_7_), channel_id=1, source_target_pairs={{0,3},{1,0},{2,1},{3,2},{4,7},{5,4},{6,5},{7,6},{8,11},{9,8},{10,9... | collective-permute-start | bytes 1572872 | tf_op jit(solution)/shard_map/ppermute | solution.py:38
  200.0 5.3 %collective-permute-start.18 = (bf16[2,4,256,256]{3,2,1,0:T(8,128)(2,1)S(1)}, bf16[2,4,256,256]{3,2,1,0:T(8,128)(2,1)S(1)}, u32[]{:S(2)}, u32[]{:S(2)}) collective-permute-start(bf16[2,4,256,256]{3,2,1,0:T(8,128)(2,1)S(1)} %get-tuple-element.88), channel_id=1, source_target_pairs={{0,16},{16,0},{32,48},{48,32},{64,80},{80,64},{96,112},{112,96},{1... | collective-permute-start | bytes 3145736 | tf_op jit(solution)/shard_map/ppermute | solution.py:561
  206.0 4.9 %collective-permute-start.21 = (bf16[256,256]{1,0:T(8,128)(2,1)S(1)}, bf16[256,256]{1,0:T(8,128)(2,1)S(1)}, u32[]{:S(2)}, u32[]{:S(2)}) collective-permute-start(bf16[256,256]{1,0:T(8,128)(2,1)S(1)} %get-tuple-element.92), channel_id=1, source_target_pairs={{0,96},{16,112},{32,0},{48,16},{64,32},{80,48},{96,64},{112,80},{1... | collective-permute-start | bytes 393224 | tf_op jit(solution)/shard_map/ppermute | solution.py:563
  207.4 5.9 %collective-permute-start.20 = (bf16[256,256]{1,0:T(8,128)(2,1)S(1)}, bf16[256,256]{1,0:T(8,128)(2,1)S(1)}, u32[]{:S(2)}, u32[]{:S(2)}) collective-permute-start(bf16[256,256]{1,0:T(8,128)(2,1)S(1)} %get-tuple-element.91), channel_id=1, source_target_pairs={{0,64},{16,80},{32,96},{48,112},{64,0},{80,16},{96,32},{112,48},{1... | collective-permute-start | bytes 393224 | tf_op jit(solution)/shard_map/ppermute | solution.py:563
  207.9 9.3 %collective-permute-start.19 = (bf16[256,256]{1,0:T(8,128)(2,1)S(1)}, bf16[256,256]{1,0:T(8,128)(2,1)S(1)}, u32[]{:S(2)}, u32[]{:S(2)}) collective-permute-start(bf16[256,256]{1,0:T(8,128)(2,1)S(1)} %get-tuple-element.90), channel_id=1, source_target_pairs={{0,32},{16,48},{32,64},{48,80},{64,96},{80,112},{96,0},{112,16},{1... | collective-permute-start | bytes 393224 | tf_op jit(solution)/shard_map/ppermute | solution.py:563
  (12 other events, 67.9 us)
